TPU v7x, 256 devices: a whole 4x4x8 slice. The times are simulated.
256 devices in a mesh: table: 32 (over z, x), scal: 8 (over y, core).
Axes of the slice: x: 4, y: 4, z: 8, core: 2. Of those that a mesh axis runs over, the one named last changes fastest.
Arguments:
- cell_coords: float32 [4, 524288], P(None, ('table', 'scal')), may hold values from 0 to 1
- flamelet_table: float32 [131072, 1024], P('table', 'scal'), may hold values from -15 to 15
- owner_shard: int32 [524288, 1], P(('table', 'scal')), may hold values from 0 to 31; in each aligned block of 64 rows (0 to 63, 64 to 127, ...) at most 5 rows name the same one
- local_bin: int32 [524288], P(('table', 'scal')), may hold values from 0 to 4095
Outputs:
- filtered_fields: float32 [32, 2048, 256], P(None, ('table', 'scal'))
- x_gradient: float32 [32, 2048, 256], P(None, ('table', 'scal'))
Inputs may be any that keep to these rules, and one draw needn't show every extreme that they name: `owner_shard`: in each aligned block of 64 rows (one group of one device's cells) no shard is named by more than 5 rows, a bound that some block reaches.
All inputs are finite; a program needn't handle non-finite values.
Results may differ from a plain program's by a relative error of at most 0.00012.
Values sent between devices are 32-bit elements; how exact they have to be, the bound alone decides.
A program may use at most 128 MiB of HBM per device.

v0:
```python
import jax
import jax.numpy as jnp
import numpy as np
from jax import lax
from jax.sharding import PartitionSpec as P

SCAL_ALL = 32
K = 32
BX = 8
LG = 8
strength = 0.499


def spline_weights(coords):
    linear = [jnp.stack([1.0 - coords[axis_id], coords[axis_id]]) for axis_id in range(3)]
    frac_last = coords[3]
    square = frac_last * frac_last
    cube = square * frac_last
    remain = 1.0 - frac_last
    cubic = jnp.stack(
        [
            remain * remain * remain / 6.0,
            (3.0 * cube - 6.0 * square + 4.0) / 6.0,
            (-3.0 * cube + 3.0 * square + 3.0 * frac_last + 1.0) / 6.0,
            cube / 6.0,
        ]
    )
    product = (
        linear[0][:, None, None, None, :]
        * linear[1][None, :, None, None, :]
        * linear[2][None, None, :, None, :]
        * cubic[None, None, None, :, :]
    )
    return product.reshape(-1, coords.shape[1])


def thomas_solve(below, middle, above, right_side):
    length = middle.shape[0]
    upper_factor = np.zeros(length)
    solved = np.zeros(right_side.shape)
    for row in range(length):
        if row == 0:
            denom = middle[0]
            solved[0] = right_side[0] / denom
        else:
            denom = middle[row] - below[row] * upper_factor[row - 1]
            solved[row] = (right_side[row] - below[row] * solved[row - 1]) / denom
        upper_factor[row] = above[row] / denom
    for row in range(length - 2, -1, -1):
        solved[row] = solved[row] - upper_factor[row] * solved[row + 1]
    return solved


def filter_table(length):
    positions = np.arange(length)
    offset = positions[None, :] - positions[:, None]
    distance = np.abs(offset)
    interior = (positions >= 3) & (positions <= length - 4)
    coeffs = [
        (11.0 + 10.0 * strength) / 16.0,
        (15.0 + 34.0 * strength) / 64.0,
        (-3.0 + 6.0 * strength) / 32.0,
        (1.0 - 2.0 * strength) / 64.0,
    ]
    band = np.zeros((length, length))
    for reach in range(4):
        band = band + np.where(distance == reach, coeffs[reach], 0.0)
    right_side = np.where(interior[:, None], band, np.where(offset == 0, 1.0, 0.0))
    coupling = np.where(interior, strength, 0.0)
    return thomas_solve(coupling, np.ones(length), coupling, right_side).astype(np.float32)


def derivative_table(length):
    positions = np.arange(length)
    offset = positions[None, :] - positions[:, None]
    distance = np.abs(offset)
    direction = np.sign(offset) * 1.0
    boundary = (positions == 0) | (positions == length - 1)
    second = (positions == 1) | (positions == length - 2)
    interior = ~(boundary | second)
    below_diag = np.where(
        interior, 1.0 / 3.0, np.where(second, 0.25, np.where(positions == length - 1, 2.0, 0.0))
    )
    above_diag = np.where(
        interior, 1.0 / 3.0, np.where(second, 0.25, np.where(positions == 0, 2.0, 0.0))
    )
    inner_rows = direction * (
        np.where(distance == 1, 7.0 / 9.0, 0.0) + np.where(distance == 2, 1.0 / 36.0, 0.0)
    )
    second_rows = direction * np.where(distance == 1, 0.75, 0.0)
    first_row = np.where(
        offset == 0, -2.5, np.where(offset == 1, 2.0, np.where(offset == 2, 0.5, 0.0))
    )
    final_row = np.where(
        offset == 0, 2.5, np.where(offset == -1, -2.0, np.where(offset == -2, -0.5, 0.0))
    )
    right_side = np.where(
        interior[:, None],
        inner_rows,
        np.where(
            second[:, None], second_rows, np.where((positions == 0)[:, None], first_row, final_row)
        ),
    )
    return thomas_solve(below_diag, np.ones(length), above_diag, right_side).astype(np.float32)


def on_device(cell_coords, flamelet_table, owner_shard, local_bin):
    table_count = lax.axis_size("table")
    scal_count = lax.axis_size("scal")
    cell_count = cell_coords.shape[1]
    group_size = cell_count // table_count
    capacity = max(2, 5 * group_size // (2 * table_count))
    slot_count = table_count * table_count * capacity
    group_slots = table_count * capacity
    owners = owner_shard[:, 0].reshape(table_count, group_size)
    matches = (
        owners[:, :, None] == jnp.arange(table_count, dtype=jnp.int32)[None, None, :]
    ).astype(jnp.int32)
    group_rank = jnp.sum((jnp.cumsum(matches, axis=1) - 1) * matches, axis=2)
    local_slot = owners * capacity + group_rank
    slot_ids = jnp.arange(group_slots, dtype=jnp.int32)
    placing = (local_slot[:, :, None] == slot_ids[None, None, :]).astype(jnp.float32)
    payload = jnp.concatenate(
        [local_bin.astype(jnp.float32)[None, :], cell_coords], axis=0
    ).reshape(5, table_count, group_size)
    placed = jnp.einsum("fgc,gcq->fgq", payload, placing, precision=lax.Precision.HIGHEST)
    outgoing = (
        placed.reshape(5, table_count, table_count, capacity)
        .transpose(0, 2, 1, 3)
        .reshape(5, table_count, group_slots)
    )
    received = lax.all_to_all(outgoing, "table", split_axis=1, concat_axis=1, tiled=True).reshape(
        5, slot_count
    )
    shard_piece = lax.all_gather(received, "scal", axis=1, tiled=True)
    weights = spline_weights(shard_piece[1:])
    table_rows = jnp.take(flamelet_table, shard_piece[0].astype(jnp.int32), axis=0)
    table_rows = table_rows.reshape(table_rows.shape[0], -1, K)
    looked = jnp.einsum("nsk,kn->sn", table_rows, weights, precision=lax.Precision.HIGHEST)
    looked = looked.reshape(looked.shape[0], scal_count, slot_count)
    grouped = lax.all_to_all(looked, "scal", split_axis=1, concat_axis=0, tiled=True).reshape(
        SCAL_ALL, table_count, table_count, capacity
    )
    length = BX * table_count
    replies = lax.all_to_all(grouped, "table", split_axis=1, concat_axis=1, tiled=True)
    by_group = replies.transpose(0, 2, 1, 3).reshape(SCAL_ALL, table_count, group_slots)
    values = jnp.einsum("sgq,gcq->sgc", by_group, placing, precision=lax.Precision.HIGHEST).reshape(
        SCAL_ALL, table_count, LG, BX
    )
    pencil = lax.all_to_all(values, "table", split_axis=1, concat_axis=3, tiled=True).reshape(
        SCAL_ALL * LG, length
    )
    filter_op = jnp.asarray(filter_table(length).T)
    derivative_op = jnp.asarray(derivative_table(length).T)
    filtered = jnp.dot(pencil, filter_op, precision=lax.Precision.HIGHEST)
    gradient = jnp.dot(filtered, derivative_op, precision=lax.Precision.HIGHEST)
    return (filtered.reshape(SCAL_ALL, LG, length), gradient.reshape(SCAL_ALL, LG, length))


def solution(mesh):
    return jax.shard_map(
        on_device,
        mesh=mesh,
        in_specs=(
            P(None, ("table", "scal")),
            P("table", "scal"),
            P(("table", "scal"), None),
            P(("table", "scal")),
        ),
        out_specs=(P(None, ("table", "scal"), None), P(None, ("table", "scal"), None)),
        check_vma=False,
    )
```

profile of v0, /device:TPU:8, one launch (start us, length us, event | category | flops | bytes accessed | tf_op | source)
XLA Modules:
  0.0 340.3 jit_solution(11872699540350610518)
XLA Ops:
  1.2 1.5 reduce.5
  2.8 1.7 select_reduce_fusion
  8.5 21.4 %all_to_all.40 = f32[32,1,800]{2,1,0:T(1,128)S(1)} all-to-all(f32[32,1,800]{2,1,0:T(1,128)S(1)} %reshape.131), channel_id=1, replica_groups=mesh['table'=32,'scal'=8] {'table'}, dimensions={0} | all-to-all | bytes 204800 | tf_op jit(solution)/shard_map/all_to_all | solution.py:132
  31.8 14.7 %all_gather.3 = f32[5,40960]{1,0:T(8,128)S(1)} all-gather(f32[5,5120]{1,0:T(8,128)S(1)} %reshape.104), channel_id=1, replica_groups=mesh['table'=32,'scal'=8] {'scal'}, dimensions={1}, use_global_device_ids=true | all-gather | bytes 921600 | tf_op jit(solution)/shard_map/all_gather | solution.py:135
  46.7 2.4 slice_convert_fusion
  49.1 134.9 %gather_fusion = f32[40960,128]{1,0:T(8,128)} fusion(f32[4096,128]{1,0:T(8,128)S(1)} %copy-done, s32[40960]{0:T(1024)S(1)} %broadcast_clamp_fusion), kind=kCustom, calls=%fused_computation | custom fusion | bytes 42106880 | tf_op jit(solution)/shard_map/jit(_take)/gather | solution.py:137
  184.1 21.2 %copy.79 = f32[40960,128]{0,1:T(8,128)} copy(f32[40960,128]{1,0:T(8,128)} %gather_fusion) | data formatting | bytes 41943040 | tf_op jit(solution)/shard_map/jit(_take)/gather | solution.py:137
  207.6 3.4 %broadcast_multiply_fusion = f32[2,2,2,4,40960]{4,3,2,1,0:T(4,128)} fusion(f32[4,40960]{1,0:T(4,128)S(1)} %pad_maximum_fusion, f32[2,2,2,40960]{3,2,1,0:T(2,128)S(1)} %broadcast_multiply_fusion.1), kind=kLoop, calls=%fused_computation.2 | loop fusion | flops 1310720 | bytes 7208960 | tf_op jit(solution)/shard_map/mul | solution.py:29
  211.0 6.1 %mul.131 = f32[32,40960]{1,0:T(8,128)} reshape(f32[2,2,2,4,40960]{4,3,2,1,0:T(4,128)} %broadcast_multiply_fusion) | data formatting | bytes 10485760 | tf_op jit(solution)/shard_map/mul | solution.py:29
  217.2 10.2 %multiply_reduce_fusion = f32[40960,4]{0,1:T(4,128)S(1)} fusion(f32[40960,4,32]{0,2,1:T(8,128)} %bitcast.56, f32[40960,32]{0,1:T(8,128)} %bitcast.57, pred[40960]{0:T(1024)(128)(4,1)S(1)} %compare_and_fusion), kind=kLoop, calls=%fused_computation.1 | loop fusion | flops 15564800 | bytes 26910720 | tf_op jit(solution)/shard_map/nsk,kn->sn/dot_general | solution.py:139
  227.4 14.6 %all_to_all.41 = f32[4,8,5120]{2,0,1:T(4,128)S(1)} all-to-all(f32[4,8,5120]{2,0,1:T(4,128)S(1)} %bitcast.60), channel_id=1, replica_groups=mesh['table'=32,'scal'=8] {'scal'}, dimensions={1} | all-to-all | bytes 1310720 | tf_op jit(solution)/shard_map/all_to_all | solution.py:141
  242.0 17.7 %reshape.106 = f32[32,32,32,5]{3,2,1,0:T(8,128)} reshape(f32[8,4,1,5120]{3,1,0,2:T(4,128)S(1)} %bitcast.61) | data formatting | bytes 1310720 | tf_op jit(solution)/shard_map/reshape | solution.py:141
  259.7 12.5 %copy.81 = f32[32,32,32,5]{2,0,3,1:T(8,128)} copy(f32[32,32,32,5]{3,2,1,0:T(8,128)} %reshape.106) | data formatting | bytes 1310720 | tf_op jit(solution)/shard_map/reshape | solution.py:141
  272.3 2.7 reshape.133
  275.0 23.3 %all_to_all.42 = f32[32,1,5120]{2,1,0:T(1,128)S(1)} all-to-all(f32[32,1,5120]{2,1,0:T(1,128)S(1)} %reshape.133), channel_id=1, replica_groups=mesh['table'=32,'scal'=8] {'table'}, dimensions={0} | all-to-all | bytes 1310720 | tf_op jit(solution)/shard_map/all_to_all | solution.py:145
  298.3 2.2 reduce.7
  300.5 2.4 reshape.134
  302.9 3.0 copy.82
  305.9 1.5 fusion.2
  308.3 17.0 %all_to_all.43 = f32[32,1,2048]{2,1,0:T(1,128)S(1)} all-to-all(f32[32,1,2048]{2,1,0:T(1,128)S(1)} %reshape.135), channel_id=1, replica_groups=mesh['table'=32,'scal'=8] {'table'}, dimensions={0} | all-to-all | bytes 524288 | tf_op jit(solution)/shard_map/all_to_all | solution.py:150
  326.7 1.3 reshape.136
  328.0 1.4 bitcast_bitcast_fusion
  329.5 4.3 %copy.85 = f32[32,1,8,32,8]{4,3,2,0,1:T(8,128)} copy(f32[32,1,8,32,8]{0,4,2,3,1:T(8,128)S(1)} %bitcast_bitcast_fusion) | data formatting | bytes 524288 | tf_op jit(solution)/shard_map/all_to_all | solution.py:150
  333.8 4.0 %reshape.109 = f32[256,256]{1,0:T(8,128)S(1)} reshape(f32[32,1,8,32,8]{4,3,2,0,1:T(8,128)} %copy.85) | data formatting | bytes 524288 | tf_op jit(solution)/shard_map/reshape | solution.py:150
  (51 shorter events, 13.7 us)
Async XLA Ops:
  0.6 48.5 %copy-start = (f32[4096,128]{1,0:T(8,128)S(1)}, f32[4096,128]{1,0:T(8,128)}, u32[]{:S(2)}) copy-start(f32[4096,128]{1,0:T(8,128)} %param.7) | copy-start | bytes 6291460
  184.1 21.2 %copy-start.4 = (f32[1,40960]{1,0:T(1,128)S(1)}, f32[1,40960]{1,0:T(1,128)}, u32[]{:S(2)}) copy-start(f32[1,40960]{1,0:T(1,128)} %get-tuple-element.5) | copy-start | bytes 491524
  184.1 21.2 %copy-start.5 = (f32[1,40960]{1,0:T(1,128)S(1)}, f32[1,40960]{1,0:T(1,128)}, u32[]{:S(2)}) copy-start(f32[1,40960]{1,0:T(1,128)} %get-tuple-element.10) | copy-start | bytes 491524
  184.1 21.5 %copy-start.3 = (f32[1,40960]{1,0:T(1,128)S(1)}, f32[1,40960]{1,0:T(1,128)}, u32[]{:S(2)}) copy-start(f32[1,40960]{1,0:T(1,128)} %get-tuple-element.12) | copy-start | bytes 491524
  211.0 6.1 %copy-start.6 = (s32[1,40960]{1,0:T(1,128)S(1)}, s32[1,40960]{1,0:T(1,128)}, u32[]{:S(2)}) copy-start(s32[1,40960]{1,0:T(1,128)} %get-tuple-element.2) | copy-start | bytes 491524
  328.0 12.3 %copy-start.1 = (f32[4096,128]{1,0:T(8,128)S(1)}, f32[4096,128]{1,0:T(8,128)}, u32[]{:S(2)}) copy-start(f32[4096,128]{1,0:T(8,128)} %param.7) | copy-start | bytes 6291460
  329.4 9.7 %copy-start.7 = (f32[256,256]{1,0:T(8,128)S(1)}, f32[256,256]{1,0:T(8,128)}, u32[]{:S(2)}) copy-start(f32[256,256]{1,0:T(8,128)} %constant.46.clone) | copy-start | bytes 786436
  339.2 1.1 copy-start.2
where the time goes:
time: 341 us; the launch traced here: 340 us
  local copies, waits for them, and re-layouts  216 us (63%)
  blocking collectives  91.1 us (27%)
  other arithmetic  27 us (8%)
  matrix products  4.91 us (1%)
    gather x2, local copies, waits for them, and re-layouts, on_device(): jnp.take(flamelet_table, shard_piece[0].astype(jnp.int32), axis=0)  156 us
    reshape x2, local copies, waits for them, and re-layouts, on_device(): lax.all_to_all(looked, 'scal', split_axis=1, concat_axis=0, tiled=True)  30.2 us
    all_to_all x1, blocking collectives, on_device(): lax.all_to_all(grouped, 'table', split_axis=1, concat_axis=1, tiled=True)  23.3 us
    all_to_all x1, blocking collectives, on_device(): lax.all_to_all(outgoing, 'table', split_axis=1, concat_axis=1, tiled=True)  21.4 us
    all_to_all x1, blocking collectives, on_device(): lax.all_to_all(values, 'table', split_axis=1, concat_axis=3, tiled=True)  17 us
    all_gather x1, blocking collectives, on_device(): shard_piece = lax.all_gather(received, 'scal', axis=1, tiled=True)  14.7 us
    all_to_all x1, blocking collectives, on_device(): lax.all_to_all(looked, 'scal', split_axis=1, concat_axis=0, tiled=True)  14.6 us
    dot_general x1, other arithmetic, on_device(): jnp.einsum('nsk,kn->sn', table_rows, weights, precision=lax.Precision.HIG...  10.2 us

commit v1 on v0

--- a/solution.py
+++ b/solution.py
@@ -138,9 +138,10 @@
     table_rows = table_rows.reshape(table_rows.shape[0], -1, K)
     looked = jnp.einsum("nsk,kn->sn", table_rows, weights, precision=lax.Precision.HIGHEST)
     looked = looked.reshape(looked.shape[0], scal_count, slot_count)
-    grouped = lax.all_to_all(looked, "scal", split_axis=1, concat_axis=0, tiled=True).reshape(
-        SCAL_ALL, table_count, table_count, capacity
-    )
+    grouped = jnp.concatenate(
+        lax.all_to_all(jnp.stack(jnp.split(looked, lax.axis_size("scal"), axis=1)), "scal", 0, 0),
+        axis=0,
+    ).reshape(SCAL_ALL, table_count, table_count, capacity)
     length = BX * table_count
     replies = lax.all_to_all(grouped, "table", split_axis=1, concat_axis=1, tiled=True)
     by_group = replies.transpose(0, 2, 1, 3).reshape(SCAL_ALL, table_count, group_slots)

time: 341 us -> 344 us (level)
    another operation x0 -> x3, local copies, waits for them, and re-layouts: none -> 30.3 us  [the longest x2 30.2 us: on_device(): grouped = jnp.concatenate(lax.all_to_all(jnp.stack(jnp.split(looked, lax....]
    reshape x2 -> x0, local copies, waits for them, and re-layouts: 30.2 us -> none  [on_device(): lax.all_to_all(looked, 'scal', split_axis=1, concat_axis=0, tiled=True)]
    unnamed x24 -> x32, local copies, waits for them, and re-layouts: 7.82 us -> 8.73 us
where the time goes in v1:
time: 344 us; the launch traced here: 343 us
  local copies, waits for them, and re-layouts  217 us (63%)
  blocking collectives  91.1 us (26%)
  other arithmetic  28.8 us (8%)
  matrix products  4.91 us (1%)
    gather x2, local copies, waits for them, and re-layouts, on_device(): jnp.take(flamelet_table, shard_piece[0].astype(jnp.int32), axis=0)  156 us
    another operation x2, local copies, waits for them, and re-layouts, on_device(): grouped = jnp.concatenate(lax.all_to_all(jnp.stack(jnp.split(looked, lax....  30.2 us
    all_to_all x1, blocking collectives, on_device(): lax.all_to_all(grouped, 'table', split_axis=1, concat_axis=1, tiled=True)  23.3 us
    all_to_all x1, blocking collectives, on_device(): lax.all_to_all(outgoing, 'table', split_axis=1, concat_axis=1, tiled=True)  21.4 us
    all_to_all x1, blocking collectives, on_device(): lax.all_to_all(values, 'table', split_axis=1, concat_axis=3, tiled=True)  17 us
    all_gather x1, blocking collectives, on_device(): shard_piece = lax.all_gather(received, 'scal', axis=1, tiled=True)  14.7 us
    all_to_all x1, blocking collectives, on_device(): lax.all_to_all(jnp.stack(jnp.split(looked, lax.axis_size('scal'), axis=1)...  14.6 us
    dot_general x1, other arithmetic, on_device(): jnp.einsum('nsk,kn->sn', table_rows, weights, precision=lax.Precision.HIG...  10.2 us

profile of v1, /device:TPU:8, one launch (start us, length us, event | category | flops | bytes accessed | tf_op | source)
XLA Modules:
  0.0 343.2 jit_solution(8099907757003795867)
XLA Ops:
  1.2 1.5 reduce.6
  2.8 1.7 select_reduce_fusion
  8.5 21.4 %all_to_all.30 = f32[32,1,800]{2,1,0:T(1,128)S(1)} all-to-all(f32[32,1,800]{2,1,0:T(1,128)S(1)} %reshape.127), channel_id=1, replica_groups=mesh['table'=32,'scal'=8] {'table'}, dimensions={0} | all-to-all | bytes 204800 | tf_op jit(solution)/shard_map/all_to_all | solution.py:132
  31.8 14.7 %all_gather.3 = f32[5,40960]{1,0:T(8,128)S(1)} all-gather(f32[5,5120]{1,0:T(8,128)S(1)} %reshape.100), channel_id=1, replica_groups=mesh['table'=32,'scal'=8] {'scal'}, dimensions={1}, use_global_device_ids=true | all-gather | bytes 921600 | tf_op jit(solution)/shard_map/all_gather | solution.py:135
  46.7 2.4 slice_convert_fusion
  49.1 134.9 %gather_fusion = f32[40960,128]{1,0:T(8,128)} fusion(f32[4096,128]{1,0:T(8,128)S(1)} %copy-done, s32[40960]{0:T(1024)S(1)} %broadcast_clamp_fusion), kind=kCustom, calls=%fused_computation | custom fusion | bytes 42106880 | tf_op jit(solution)/shard_map/jit(_take)/gather | solution.py:137
  184.1 21.2 %copy.82 = f32[40960,128]{0,1:T(8,128)} copy(f32[40960,128]{1,0:T(8,128)} %gather_fusion) | data formatting | bytes 41943040 | tf_op jit(solution)/shard_map/jit(_take)/gather | solution.py:137
  207.6 3.4 broadcast_multiply_fusion
  211.0 6.1 %mul.131 = f32[32,40960]{1,0:T(8,128)} reshape(f32[2,2,2,4,40960]{4,3,2,1,0:T(4,128)} %broadcast_multiply_fusion) | data formatting | bytes 10485760 | tf_op jit(solution)/shard_map/mul | solution.py:29
  217.2 10.2 %multiply_reduce_fusion = f32[40960,4]{0,1:T(4,128)S(1)} fusion(f32[40960,4,32]{0,2,1:T(8,128)} %bitcast.85, f32[40960,32]{0,1:T(8,128)} %bitcast.86, pred[40960]{0:T(1024)(128)(4,1)S(1)} %compare_and_fusion), kind=kLoop, calls=%fused_computation.1 | loop fusion | flops 15564800 | bytes 26910720 | tf_op jit(solution)/shard_map/nsk,kn->sn/dot_general | solution.py:139
  228.5 14.6 %all_to_all.31 = f32[8,4,1,5120]{3,2,1,0:T(1,128)S(1)} all-to-all(f32[8,4,1,5120]{3,2,1,0:T(1,128)S(1)} %fusion.13), channel_id=1, replica_groups=mesh['table'=32,'scal'=8] {'scal'}, dimensions={0} | all-to-all | bytes 1310720 | tf_op jit(solution)/shard_map/all_to_all | solution.py:142
  243.1 1.8 reduce.2
  244.9 17.7 %reshape_reshape.3 = f32[32,32,32,5]{3,2,1,0:T(8,128)} reshape(f32[8,4,5120]{2,1,0:T(4,128)S(1)} %reduce.2) | data formatting | bytes 1310720 | tf_op jit(solution)/shard_map/reshape;reshape | solution.py:144
  262.6 12.5 %copy.83 = f32[32,32,32,5]{2,0,3,1:T(8,128)} copy(f32[32,32,32,5]{3,2,1,0:T(8,128)} %reshape_reshape.3) | data formatting | bytes 1310720 | tf_op jit(solution)/shard_map/reshape;reshape | solution.py:144
  275.1 2.7 reshape.129
  277.8 23.3 %all_to_all.32 = f32[32,1,5120]{2,1,0:T(1,128)S(1)} all-to-all(f32[32,1,5120]{2,1,0:T(1,128)S(1)} %reshape.129), channel_id=1, replica_groups=mesh['table'=32,'scal'=8] {'table'}, dimensions={0} | all-to-all | bytes 1310720 | tf_op jit(solution)/shard_map/all_to_all | solution.py:146
  301.2 2.2 reduce.8
  303.4 2.4 reshape.130
  305.8 3.0 copy.84
  308.8 1.5 fusion.2
  311.2 17.0 %all_to_all.33 = f32[32,1,2048]{2,1,0:T(1,128)S(1)} all-to-all(f32[32,1,2048]{2,1,0:T(1,128)S(1)} %reshape.131), channel_id=1, replica_groups=mesh['table'=32,'scal'=8] {'table'}, dimensions={0} | all-to-all | bytes 524288 | tf_op jit(solution)/shard_map/all_to_all | solution.py:151
  330.9 1.4 bitcast_bitcast_fusion
  332.3 4.3 %copy.87 = f32[32,1,8,32,8]{4,3,2,0,1:T(8,128)} copy(f32[32,1,8,32,8]{0,4,2,3,1:T(8,128)S(1)} %bitcast_bitcast_fusion) | data formatting | bytes 524288 | tf_op jit(solution)/shard_map/all_to_all | solution.py:151
  336.7 4.0 %reshape.104 = f32[256,256]{1,0:T(8,128)S(1)} reshape(f32[32,1,8,32,8]{4,3,2,0,1:T(8,128)} %copy.87) | data formatting | bytes 524288 | tf_op jit(solution)/shard_map/reshape | solution.py:151
  (61 shorter events, 16.1 us)
Async XLA Ops:
  0.6 48.5 %copy-start = (f32[4096,128]{1,0:T(8,128)S(1)}, f32[4096,128]{1,0:T(8,128)}, u32[]{:S(2)}) copy-start(f32[4096,128]{1,0:T(8,128)} %param.7) | copy-start | bytes 6291460
  184.1 21.2 %copy-start.4 = (f32[1,40960]{1,0:T(1,128)S(1)}, f32[1,40960]{1,0:T(1,128)}, u32[]{:S(2)}) copy-start(f32[1,40960]{1,0:T(1,128)} %get-tuple-element.5) | copy-start | bytes 491524
  184.1 21.2 %copy-start.5 = (f32[1,40960]{1,0:T(1,128)S(1)}, f32[1,40960]{1,0:T(1,128)}, u32[]{:S(2)}) copy-start(f32[1,40960]{1,0:T(1,128)} %get-tuple-element.10) | copy-start | bytes 491524
  184.1 21.5 %copy-start.3 = (f32[1,40960]{1,0:T(1,128)S(1)}, f32[1,40960]{1,0:T(1,128)}, u32[]{:S(2)}) copy-start(f32[1,40960]{1,0:T(1,128)} %get-tuple-element.12) | copy-start | bytes 491524
  211.0 6.1 %copy-start.6 = (s32[1,40960]{1,0:T(1,128)S(1)}, s32[1,40960]{1,0:T(1,128)}, u32[]{:S(2)}) copy-start(s32[1,40960]{1,0:T(1,128)} %get-tuple-element.2) | copy-start | bytes 491524
  330.9 12.3 %copy-start.1 = (f32[4096,128]{1,0:T(8,128)S(1)}, f32[4096,128]{1,0:T(8,128)}, u32[]{:S(2)}) copy-start(f32[4096,128]{1,0:T(8,128)} %param.7) | copy-start | bytes 6291460
  332.3 9.7 %copy-start.7 = (f32[256,256]{1,0:T(8,128)S(1)}, f32[256,256]{1,0:T(8,128)}, u32[]{:S(2)}) copy-start(f32[256,256]{1,0:T(8,128)} %constant.46.clone) | copy-start | bytes 786436
  342.1 1.1 copy-start.2
